TPU v7x, 512 devices: a whole 4x4x16 slice. The times are simulated.
512 devices in a mesh: expert: 32 (over x, y, core), tensor: 16 (over z).
Axes of the slice: x: 4, y: 4, z: 16, core: 2. Of those that a mesh axis runs over, the one named last changes fastest.
Arguments:
- tokens: bfloat16 [1024, 7168], P('expert', 'tensor'), may hold values from -6 to 6
- expert_ids: int32 [1024, 8], P('expert'), may hold values from 0 to 31, all different within a row; in each aligned block of 32 rows (0 to 31, 32 to 63, ...) at most 24 rows name the same one
- combine: float32 [1024, 8], P('expert'), may hold values from 0.1 to 0.5
- w_in: bfloat16 [32, 7168, 2048], P('expert', None, 'tensor'), may hold values from -0.0625 to 0.0625
- w_down: bfloat16 [32, 1024, 7168], P('expert', None, 'tensor'), may hold values from -0.1875 to 0.1875
Outputs:
- moe_out: bfloat16 [1024, 7168], P('expert', 'tensor')
Inputs may be any that keep to these rules, and one draw needn't show every extreme that they name: `expert_ids`: each row names 8 different experts. Within the 32 tokens of one index of expert, no expert is named by more than 24 rows.
All inputs are finite; a program needn't handle non-finite values.
Results may differ from a plain program's by a relative error of at most 0.008.
Values may be sent and summed in bfloat16 or wider, within the bound.
No kernel may reach another device: no remote copies, remote signals or barrier semaphores. Data moves between devices by JAX's collectives and lax.ppermute only.
A program may use at most 64 MiB of HBM per device.

v0:
```python
import jax
import jax.numpy as jnp
from jax import lax
from jax.sharding import PartitionSpec as P

TOP = 8


def route_slots(expert_ids, experts):
    one_hot = (
        expert_ids[:, :, None] == jnp.arange(experts, dtype=jnp.int32)[None, None, :]
    ).astype(jnp.int32)
    per_token = jnp.sum(one_hot, axis=1)
    before = jnp.cumsum(per_token, axis=0) - per_token
    return jnp.take_along_axis(before, expert_ids, axis=1)


def per_device(tokens, expert_ids, combine, w_in, w_down):
    experts = lax.axis_size("expert")
    tok_group = tokens.shape[0]
    capacity = min(tok_group, 3 * tok_group * TOP // experts)
    slot_index = route_slots(expert_ids, experts)
    target = (expert_ids * capacity + slot_index).reshape(-1)
    w_local = w_in[0]
    down_local = w_down[0]
    feat_width = tokens.shape[1]
    spread = jnp.repeat(tokens, TOP, axis=0)
    buffer = jnp.zeros((experts * capacity, feat_width), tokens.dtype).at[target].set(spread)
    arrived = lax.all_to_all(
        buffer.reshape(experts, capacity, feat_width),
        "expert",
        split_axis=0,
        concat_axis=0,
        tiled=True,
    )
    token_rows = arrived.reshape(experts * capacity, tokens.shape[1])
    weights = w_local
    gate_up = jnp.dot(
        lax.all_gather(token_rows, "tensor", axis=1, tiled=True),
        weights,
        preferred_element_type=jnp.float32,
    )
    half_width = w_local.shape[1] // 2
    hidden = (jax.nn.silu(gate_up[:, :half_width]) * gate_up[:, half_width:]).astype(jnp.bfloat16)
    weights = down_local
    expert_out = jnp.dot(
        lax.all_gather(hidden, "tensor", axis=1, tiled=True),
        weights,
        preferred_element_type=jnp.float32,
    ).astype(jnp.bfloat16)
    returned = lax.all_to_all(
        expert_out.reshape(experts, capacity, down_local.shape[1]),
        "expert",
        split_axis=0,
        concat_axis=0,
        tiled=True,
    )
    returned_flat = returned.reshape(experts * capacity, down_local.shape[1])
    picked = returned_flat[target].reshape(tok_group, TOP, down_local.shape[1])
    combined = jnp.einsum("tk,tkd->td", combine, picked.astype(jnp.float32))
    return combined.astype(jnp.bfloat16)


def solution(mesh):
    in_specs = (
        P("expert", "tensor"),
        P("expert", None),
        P("expert", None),
        P("expert", None, "tensor"),
        P("expert", None, "tensor"),
    )
    out_specs = P("expert", "tensor")
    return jax.shard_map(
        per_device, mesh=mesh, in_specs=in_specs, out_specs=out_specs, check_vma=False
    )
```

profile of v0, /device:TPU:1, one launch (start us, length us, event | category | flops | bytes accessed | tf_op | source)
XLA Modules:
  0.0 278.9 jit_solution(17810822857758711456)
XLA Ops:
  6.5 0.0 copy-start
  6.5 0.0 all-gather.3.cloned.1.call-start
  6.5 0.9 copy.28
  7.4 0.1 convert_reduce_fusion
  7.6 0.1 reduce_window_sum.11
  7.6 0.1 reshape.75
  7.7 0.0 copy-start.1
  7.7 1.9 gather_fusion.1
  9.7 0.1 reshape.78
  9.8 0.1 reshape.60
  9.9 0.0 copy-done.1
  9.9 1.8 scatter_custom_fusion
  11.7 23.8 %all_to_all.10 = bf16[32,24,448]{2,1,0:T(8,128)(2,1)S(1)} all-to-all(bf16[32,24,448]{2,1,0:T(8,128)(2,1)S(1)} %bitcast.29), channel_id=1, replica_groups=mesh['expert'=32,'tensor'=16] {'expert'}, dimensions={0} | all-to-all | bytes 1376256 | tf_op jit(solution)/shard_map/all_to_all | solution.py:29
  35.5 1.1 copy.33
  36.6 0.0 all-gather.3.cloned.1.call-update
  36.7 0.0 copy-start.3
  36.7 0.0 all-gather.5.cloned.1.call-start
  36.7 131.4 %all-gather.3.cloned.1.call-done = bf16[768,7168]{0,1:T(8,128)(2,1)} async-done(((bf16[768,448]{0,1:T(8,128)(2,1)}), bf16[768,7168]{0,1:T(8,128)(2,1)}) %all-gather.3.cloned.1.call-update) | async-done | bytes 11010064 | tf_op jit(solution)/shard_map/all_gather | solution.py:39
  168.1 0.0 copy-done
  168.1 5.9 %fusion = f32[768,128]{0,1:T(8,128)S(1)} fusion(bf16[768,7168]{0,1:T(8,128)(2,1)} %all-gather.3.cloned.1.call-done, bf16[1,7168,128]{2,1,0:T(8,128)(2,1)S(1)} %copy-done), kind=kOutput, calls=%fused_computation.3 | convolution fusion | flops 1409286144 | bytes 13238272 | tf_op jit(solution)/shard_map/dot_general | solution.py:38
  174.0 0.7 fusion.8
  174.7 0.0 all-gather.5.cloned.1.call-update
  174.7 60.5 %all-gather.5.cloned.1.call-done = bf16[768,1024]{0,1:T(8,128)(2,1)} async-done(((bf16[768,64]{0,1:T(8,128)(2,1)}), bf16[768,1024]{0,1:T(8,128)(2,1)}) %all-gather.5.cloned.1.call-update) | async-done | bytes 1572880 | tf_op jit(solution)/shard_map/all_gather | solution.py:47
  235.2 0.0 copy-done.3
  235.2 2.3 convolution_convert_fusion
  237.5 0.0 copy-start.2
  237.5 1.2 copy.34
  238.7 17.2 %all-to-all-start.1 = ((bf16[32,24,448]{2,1,0:T(8,128)(2,1)}), bf16[32,24,448]{2,1,0:T(8,128)(2,1)S(1)}, u32[]{:S(2)}, u32[]{:S(2)}) async-start(bf16[32,24,448]{2,1,0:T(8,128)(2,1)} %bitcast.7), calls=%async_computation.1 | async-start | bytes 1572864 | tf_op jit(solution)/shard_map/all_to_all | solution.py:51
  255.9 0.0 copy-done.2
  255.9 0.1 copy.35
  256.0 14.1 %all-to-all-done.1 = bf16[32,24,448]{2,1,0:T(8,128)(2,1)S(1)} async-done(((bf16[32,24,448]{2,1,0:T(8,128)(2,1)}), bf16[32,24,448]{2,1,0:T(8,128)(2,1)S(1)}, u32[]{:S(2)}, u32[]{:S(2)}) %all-to-all-start.1) | async-done | bytes 688160 | tf_op jit(solution)/shard_map/all_to_all | solution.py:51
  270.1 1.2 gather_fusion
  271.3 0.2 fusion.5
  271.5 0.6 copy.38
  (5 shorter events, 0.0 us)
Async XLA Ops:
  6.5 161.6 %copy-start = (bf16[1,7168,128]{2,1,0:T(8,128)(2,1)S(1)}, bf16[1,7168,128]{2,1,0:T(8,128)(2,1)}, u32[]{:S(2)}) copy-start(bf16[1,7168,128]{2,1,0:T(8,128)(2,1)} %param.8) | copy-start | bytes 5505028
  6.5 161.6 %all-gather.3.cloned.1.call-start = ((), (), s32[]{:S(2)}) async-start(), calls=%async_computation.2 | async-start | bytes 11698176 | tf_op jit(solution)/shard_map/all_gather | solution.py:39
  7.7 2.2 copy-start.1
  36.7 198.5 %copy-start.3 = (bf16[1,1024,448]{1,2,0:T(8,128)(2,1)S(1)}, bf16[1,1024,448]{1,2,0:T(8,128)(2,1)}, u32[]{:S(2)}) copy-start(bf16[1,1024,448]{1,2,0:T(8,128)(2,1)} %param.9) | copy-start | bytes 2752516
  36.7 198.5 %all-gather.5.cloned.1.call-start = ((), (), s32[]{:S(2)}) async-start(), calls=%async_computation.3 | async-start | bytes 1671168 | tf_op jit(solution)/shard_map/all_gather | solution.py:47
  237.5 18.4 %copy-start.2 = (f32[32,8]{0,1:T(8,128)S(1)}, f32[32,8]{0,1:T(8,128)}, u32[]{:S(2)}) copy-start(f32[32,8]{0,1:T(8,128)} %param.7) | copy-start | bytes 3076
  238.7 31.4 %all-to-all-start.1 = ((bf16[32,24,448]{2,1,0:T(8,128)(2,1)}), bf16[32,24,448]{2,1,0:T(8,128)(2,1)S(1)}, u32[]{:S(2)}, u32[]{:S(2)}) async-start(bf16[32,24,448]{2,1,0:T(8,128)(2,1)} %bitcast.7), calls=%async_computation.1 | async-start | bytes 1572864 | tf_op jit(solution)/shard_map/all_to_all | solution.py:51
Sparse Core Ops, SparseCore 0:
  36.8 131.3 all-gather.2
  174.8 60.2 all-gather.4
where the time goes:
time: 279 us
  waiting for transfers between devices  206 us (74%)
  blocking collectives  23.8 us (9%)
  starting transfers between devices  17.3 us (6%)
  between operations  13.5 us (5%)
  local copies, waits for them, and re-layouts  9.04 us (3%)
  matrix products  8.34 us (3%)
    all_gather x1, waiting for transfers between devices, per_device(): lax.all_gather(token_rows, 'tensor', axis=1, tiled=True)  131 us
    all_gather x1, waiting for transfers between devices, per_device(): lax.all_gather(hidden, 'tensor', axis=1, tiled=True)  60.5 us
    all_to_all x1, blocking collectives, per_device(): lax.all_to_all(buffer.reshape(experts, capacity, feat_width), 'expert', s...  23.8 us
    all_to_all x1, starting transfers between devices, per_device(): lax.all_to_all(expert_out.reshape(experts, capacity, down_local.shape[1])...  17.2 us
    all_to_all x1, waiting for transfers between devices, per_device(): lax.all_to_all(expert_out.reshape(experts, capacity, down_local.shape[1])...  14.1 us
    dot_general x1, matrix products, per_device(): jnp.dot(lax.all_gather(token_rows, 'tensor', axis=1, tiled=True), weights...  5.85 us
  transfers between devices with their start and end apart: 3, of which 3 were waited for; matrix products, arithmetic and copies ran while one was open for 0% of the time, Pallas kernels for 0%

commit v1 on v0

--- a/solution.py
+++ b/solution.py
@@ -43,11 +43,15 @@
     half_width = w_local.shape[1] // 2
     hidden = (jax.nn.silu(gate_up[:, :half_width]) * gate_up[:, half_width:]).astype(jnp.bfloat16)
     weights = down_local
-    expert_out = jnp.dot(
-        lax.all_gather(hidden, "tensor", axis=1, tiled=True),
-        weights,
-        preferred_element_type=jnp.float32,
-    ).astype(jnp.bfloat16)
+    expand_packet = lambda here_x: jnp.concatenate(
+        lax.all_to_all(
+            jnp.stack([here_x for _ in range(lax.axis_size("tensor"))], axis=0), "tensor", 0, 0
+        ),
+        1,
+    )
+    expert_out = jnp.dot(expand_packet(hidden), weights, preferred_element_type=jnp.float32).astype(
+        jnp.bfloat16
+    )
     returned = lax.all_to_all(
         expert_out.reshape(experts, capacity, down_local.shape[1]),
         "expert",

time: 279 us -> 290 us (1.039)
  blocking collectives: 23.8 us -> 100 us
  waiting for transfers between devices: 206 us -> 146 us
  starting transfers between devices: 17.3 us -> 13.8 us
    all_to_all x0 -> x1, blocking collectives: none -> 76.6 us  [per_device(): lax.all_to_all(jnp.stack([here_x for _ in range(lax.axis_size('tensor'))]...]
    all_gather x1 -> x0, waiting for transfers between devices: 60.5 us -> none  [per_device(): lax.all_gather(hidden, 'tensor', axis=1, tiled=True)]
    all_to_all x1, starting transfers between devices: 17.2 us -> 13.8 us  [per_device(): lax.all_to_all(expert_out.reshape(experts, capacity, down_local.shape[1])...]
  transfers between devices with their start and end apart: 3 -> 2, of which waited for: 3 -> 2; matrix products, arithmetic and copies ran while one was open for 0% -> 0% of each run, Pallas kernels for 0% -> 0%
where the time goes in v1:
time: 290 us
  waiting for transfers between devices  146 us (50%)
  blocking collectives  100 us (34%)
  starting transfers between devices  13.8 us (5%)
  between operations  13.5 us (5%)
  local copies, waits for them, and re-layouts  9.17 us (3%)
  matrix products  6.93 us (2%)
    all_gather x1, waiting for transfers between devices, per_device(): lax.all_gather(token_rows, 'tensor', axis=1, tiled=True)  131 us
    all_to_all x1, blocking collectives, per_device(): lax.all_to_all(jnp.stack([here_x for _ in range(lax.axis_size('tensor'))]...  76.6 us
    all_to_all x1, blocking collectives, per_device(): lax.all_to_all(buffer.reshape(experts, capacity, feat_width), 'expert', s...  23.8 us
    all_to_all x1, waiting for transfers between devices, per_device(): lax.all_to_all(expert_out.reshape(experts, capacity, down_local.shape[1])...  14.1 us
    all_to_all x1, starting transfers between devices, per_device(): lax.all_to_all(expert_out.reshape(experts, capacity, down_local.shape[1])...  13.8 us
    dot_general x1, matrix products, per_device(): jnp.dot(lax.all_gather(token_rows, 'tensor', axis=1, tiled=True), weights...  5.85 us
  transfers between devices with their start and end apart: 2, of which 2 were waited for; matrix products, arithmetic and copies ran while one was open for 0% of the time, Pallas kernels for 0%

profile of v1, /device:TPU:1, one launch (start us, length us, event | category | flops | bytes accessed | tf_op | source)
XLA Modules:
  0.0 289.8 jit_solution(1957028703330903890)
XLA Ops:
  6.5 0.0 copy-start
  6.5 0.0 all-gather.2.cloned.1.call-start
  6.5 0.9 copy.29
  7.4 0.1 convert_reduce_fusion
  7.6 0.1 reduce_window_sum.11
  7.6 0.1 reshape.85
  7.7 0.0 copy-start.1
  7.7 1.9 gather_fusion.1
  9.7 0.1 reshape.88
  9.8 0.1 reshape.68
  9.9 0.0 copy-done.1
  9.9 1.8 scatter_custom_fusion
  11.7 23.8 %all_to_all.15 = bf16[32,24,448]{2,1,0:T(8,128)(2,1)S(1)} all-to-all(bf16[32,24,448]{2,1,0:T(8,128)(2,1)S(1)} %bitcast.32), channel_id=1, replica_groups=mesh['expert'=32,'tensor'=16] {'expert'}, dimensions={0} | all-to-all | bytes 1376256 | tf_op jit(solution)/shard_map/all_to_all | solution.py:29
  35.5 1.1 copy.34
  36.6 0.0 all-gather.2.cloned.1.call-update
  36.7 131.5 %all-gather.2.cloned.1.call-done = bf16[768,7168]{0,1:T(8,128)(2,1)} async-done(((bf16[768,448]{0,1:T(8,128)(2,1)}), bf16[768,7168]{0,1:T(8,128)(2,1)}) %all-gather.2.cloned.1.call-update) | async-done | bytes 11010064 | tf_op jit(solution)/shard_map/all_gather | solution.py:39
  168.1 0.0 copy-done
  168.1 5.8 %fusion = f32[768,128]{0,1:T(8,128)S(1)} fusion(bf16[768,7168]{0,1:T(8,128)(2,1)} %all-gather.2.cloned.1.call-done, bf16[1,7168,128]{2,1,0:T(8,128)(2,1)S(1)} %copy-done), kind=kOutput, calls=%fused_computation.3 | convolution fusion | flops 1409286144 | bytes 13238272 | tf_op jit(solution)/shard_map/dot_general | solution.py:38
  174.0 0.1 fusion.8
  174.1 0.1 stack.2
  174.2 0.0 copy-start.3
  174.2 76.6 %all_to_all.16 = bf16[16,768,64]{1,2,0:T(8,128)(2,1)S(1)} all-to-all(bf16[16,768,64]{1,2,0:T(8,128)(2,1)S(1)} %stack.2), channel_id=1, replica_groups=mesh['expert'=32,'tensor'=16] {'tensor'}, dimensions={0} | all-to-all | bytes 3145728 | tf_op jit(solution)/shard_map/all_to_all | solution.py:47
  250.8 0.0 copy-done.3
  250.8 0.9 convolution_convert_fusion
  251.7 0.0 copy-start.2
  251.7 1.2 copy.35
  252.9 13.8 %all-to-all-start.2 = ((bf16[32,24,448]{2,1,0:T(8,128)(2,1)}), bf16[32,24,448]{2,1,0:T(8,128)(2,1)S(1)}, u32[]{:S(2)}, u32[]{:S(2)}) async-start(bf16[32,24,448]{2,1,0:T(8,128)(2,1)} %bitcast.9), calls=%async_computation.2 | async-start | bytes 1572864 | tf_op jit(solution)/shard_map/all_to_all | solution.py:55
  266.7 0.0 copy-done.2
  266.7 0.1 copy.36
  266.8 14.1 %all-to-all-done.2 = bf16[32,24,448]{2,1,0:T(8,128)(2,1)S(1)} async-done(((bf16[32,24,448]{2,1,0:T(8,128)(2,1)}), bf16[32,24,448]{2,1,0:T(8,128)(2,1)S(1)}, u32[]{:S(2)}, u32[]{:S(2)}) %all-to-all-start.2) | async-done | bytes 688160 | tf_op jit(solution)/shard_map/all_to_all | solution.py:55
  281.0 1.2 gather_fusion
  282.1 0.2 fusion.5
  282.3 0.6 copy.39
  (5 shorter events, 0.0 us)
Async XLA Ops:
  6.5 161.6 %copy-start = (bf16[1,7168,128]{2,1,0:T(8,128)(2,1)S(1)}, bf16[1,7168,128]{2,1,0:T(8,128)(2,1)}, u32[]{:S(2)}) copy-start(bf16[1,7168,128]{2,1,0:T(8,128)(2,1)} %param.8) | copy-start | bytes 5505028
  6.5 161.6 %all-gather.2.cloned.1.call-start = ((), (), s32[]{:S(2)}) async-start(), calls=%async_computation.3 | async-start | bytes 11698176 | tf_op jit(solution)/shard_map/all_gather | solution.py:39
  7.7 2.2 copy-start.1
  174.2 76.6 %copy-start.3 = (bf16[1,1024,448]{1,2,0:T(8,128)(2,1)S(1)}, bf16[1,1024,448]{1,2,0:T(8,128)(2,1)}, u32[]{:S(2)}) copy-start(bf16[1,1024,448]{1,2,0:T(8,128)(2,1)} %param.9) | copy-start | bytes 2752516
  251.7 15.0 %copy-start.2 = (f32[32,8]{0,1:T(8,128)S(1)}, f32[32,8]{0,1:T(8,128)}, u32[]{:S(2)}) copy-start(f32[32,8]{0,1:T(8,128)} %param.7) | copy-start | bytes 3076
  252.9 28.1 %all-to-all-start.2 = ((bf16[32,24,448]{2,1,0:T(8,128)(2,1)}), bf16[32,24,448]{2,1,0:T(8,128)(2,1)S(1)}, u32[]{:S(2)}, u32[]{:S(2)}) async-start(bf16[32,24,448]{2,1,0:T(8,128)(2,1)} %bitcast.9), calls=%async_computation.2 | async-start | bytes 1572864 | tf_op jit(solution)/shard_map/all_to_all | solution.py:55
Sparse Core Ops, SparseCore 0:
  36.8 131.3 all-gather.1
